TPU v7x, 32 devices: a whole 2x2x4 slice. The times are simulated.
32 devices in a mesh: dp: 8 (over z, x), seq: 4 (over y, core).
Axes of the slice: x: 2, y: 2, z: 4, core: 2. Of those that a mesh axis runs over, the one named last changes fastest.
Arguments:
- queries: bfloat16 [8, 512, 1024], P('dp', 'seq'), may hold values from -6 to 6
- key_vecs: bfloat16 [8, 512, 1024], P('dp', 'seq'), may hold values from -6 to 6
- value_vecs: bfloat16 [8, 512, 1024], P('dp', 'seq'), may hold values from -6 to 6
- residual_in: bfloat16 [8, 512, 1024], P('dp', 'seq'), may hold values from -8 to 8
- point_weight: bfloat16 [1024, 2048], P('seq'), may hold values from -0.5 to 0.5
- context_grad: bfloat16 [8, 512, 1024], P('dp', 'seq'), may hold values from -6 to 6
- depth_kernel: float32 [31, 1024], replicated, may hold values from -1 to 1
- norm_gain: float32 [1024], replicated, may hold values from 0.5 to 1.5
- norm_bias: float32 [1024], replicated, may hold values from -3 to 3
- conv_grad: bfloat16 [8, 512, 1024], P('dp', 'seq'), may hold values from -1.5 to 1.5
Outputs:
- context: bfloat16 [8, 512, 1024], P('dp', 'seq')
- conv_output: bfloat16 [8, 512, 1024], P('dp', 'seq')
- query_grad: bfloat16 [8, 512, 1024], P('dp', 'seq')
- key_grad: bfloat16 [8, 512, 1024], P('dp', 'seq')
- value_grad: bfloat16 [8, 512, 1024], P('dp', 'seq')
- input_grad: bfloat16 [8, 512, 2048], P('dp', 'seq')
- residual_grad: bfloat16 [8, 512, 1024], P('dp', 'seq')
- kernel_grad: float32 [31, 1024], replicated
- gain_grad: float32 [1024], replicated
- bias_grad: float32 [1024], replicated
All inputs are finite; a program needn't handle non-finite values.
Results may differ from a plain program's by a relative error of at most 0.0049.
The roundings to bfloat16 on the way count: a program that leaves them out, or rounds other values in their place, can miss the bound.
Values may be sent and summed in bfloat16 or wider, within the bound.
A program may use at most 64 MiB of HBM per device.

v0:
```python
import jax
import jax.numpy as jnp
from jax import lax
from jax.sharding import PartitionSpec as P

HEADS = 16


def from_behind(block, axis, distance):
    devices = range(lax.axis_size(axis))
    route = [(i - distance, i) for i in devices if i - distance in devices]
    return lax.ppermute(block, axis, route)


def block_probs(query_block, key_heads, scaling):
    scores = (
        jnp.einsum("qhd,khd->hqk", query_block, key_heads, preferred_element_type=jnp.float32)
        * scaling
    )
    shifted = jnp.exp(scores - jnp.max(scores, axis=2, keepdims=True))
    return shifted / jnp.sum(shifted, axis=2, keepdims=True)


def attend_forward(query_part, key_part, value_part, head_count):
    frames, channels = query_part.shape
    head_depth = channels // head_count
    scaling = head_depth ** (-0.5)
    query_heads = query_part.reshape(frames, head_count, head_depth)
    key_heads = key_part.reshape(frames, head_count, head_depth)
    value_heads = value_part.reshape(frames, head_count, head_depth)
    block_rows = min(512, frames)

    def one_block(running, index):
        query_block = lax.dynamic_slice_in_dim(query_heads, index * block_rows, block_rows, 0)
        rounded = block_probs(query_block, key_heads, scaling).astype(jnp.bfloat16)
        context = jnp.einsum(
            "hqk,khd->qhd", rounded, value_heads, preferred_element_type=jnp.float32
        ).astype(jnp.bfloat16)
        return (running, context)

    unused, blocks = lax.scan(
        one_block, jnp.zeros((), jnp.float32), jnp.arange(frames // block_rows)
    )
    return blocks.reshape(frames, channels)


def attend_backward(query_part, key_part, value_part, grad_part, context_part, head_count):
    frames, channels = query_part.shape
    head_depth = channels // head_count
    scaling = head_depth ** (-0.5)
    query_heads = query_part.reshape(frames, head_count, head_depth)
    key_heads = key_part.reshape(frames, head_count, head_depth)
    value_heads = value_part.reshape(frames, head_count, head_depth)
    grad_heads = grad_part.reshape(frames, head_count, head_depth)
    context_heads = context_part.reshape(frames, head_count, head_depth)
    block_rows = min(512, frames)

    def one_block(running, index):
        key_total, value_total = running
        start = index * block_rows
        query_block = lax.dynamic_slice_in_dim(query_heads, start, block_rows, 0)
        grad_block = lax.dynamic_slice_in_dim(grad_heads, start, block_rows, 0)
        context_block = lax.dynamic_slice_in_dim(context_heads, start, block_rows, 0)
        probabilities = block_probs(query_block, key_heads, scaling)
        rounded = probabilities.astype(jnp.bfloat16)
        row_dots = jnp.sum(
            grad_block.astype(jnp.float32) * context_block.astype(jnp.float32), axis=2
        )
        prob_grad = jnp.einsum(
            "qhd,khd->hqk", grad_block, value_heads, preferred_element_type=jnp.float32
        )
        score_grad = (probabilities * (prob_grad - row_dots.T[:, :, None]) * scaling).astype(
            jnp.bfloat16
        )
        query_grad = jnp.einsum(
            "hqk,khd->qhd", score_grad, key_heads, preferred_element_type=jnp.float32
        ).astype(jnp.bfloat16)
        key_total = key_total + jnp.einsum(
            "hqk,qhd->khd", score_grad, query_block, preferred_element_type=jnp.float32
        )
        value_total = value_total + jnp.einsum(
            "hqk,qhd->khd", rounded, grad_block, preferred_element_type=jnp.float32
        )
        return ((key_total, value_total), query_grad)

    empty = jnp.zeros((frames, head_count, head_depth), jnp.float32)
    totals, blocks = lax.scan(one_block, (empty, empty), jnp.arange(frames // block_rows))
    query_grad = blocks.reshape(frames, channels)
    key_grad = totals[0].astype(jnp.bfloat16).reshape(frames, channels)
    value_grad = totals[1].astype(jnp.bfloat16).reshape(frames, channels)
    return (query_grad, key_grad, value_grad)


def shards(
    queries,
    key_vecs,
    value_vecs,
    residual_in,
    point_weight,
    context_grad,
    depth_kernel,
    norm_gain,
    norm_bias,
    conv_grad,
):
    head_count = HEADS // lax.axis_size("seq")
    query_heads, key_heads, value_heads = (
        lax.all_to_all(queries, "seq", split_axis=2, concat_axis=1, tiled=True),
        lax.all_to_all(key_vecs, "seq", split_axis=2, concat_axis=1, tiled=True),
        lax.all_to_all(value_vecs, "seq", split_axis=2, concat_axis=1, tiled=True),
    )
    context_local = attend_forward(query_heads[0], key_heads[0], value_heads[0], head_count)
    context_out = lax.all_to_all(
        context_local[None], "seq", split_axis=1, concat_axis=2, tiled=True
    )
    taps = depth_kernel.shape[0]
    channels = depth_kernel.shape[1]
    span = taps - 1
    frames = residual_in.shape[1]
    mixed = (residual_in[0].astype(jnp.float32) + context_out[0].astype(jnp.float32)).astype(
        jnp.bfloat16
    )
    pre_conv = jnp.dot(
        mixed,
        lax.all_gather(point_weight, "seq", axis=0, tiled=True),
        preferred_element_type=jnp.float32,
    )
    conv_input = pre_conv.astype(jnp.bfloat16)[None]
    value_half = conv_input[:, :, :channels].astype(jnp.float32)
    gate_sig = jax.nn.sigmoid(conv_input[:, :, channels:].astype(jnp.float32))
    glu = (value_half * gate_sig).astype(jnp.bfloat16)
    earlier = from_behind(glu[:, frames - span :], "seq", 1)
    glu_wide = jnp.concatenate([earlier, glu], axis=1)
    glu_view = lax.optimization_barrier(glu_wide).astype(jnp.float32)
    depthwise = jnp.zeros((1, frames, channels), jnp.float32)
    for offset in range(taps):
        depthwise = depthwise + depth_kernel[offset] * glu_view[:, offset : offset + frames]
    average = jnp.mean(depthwise, axis=2, keepdims=True)
    centered = depthwise - average
    variance = jnp.mean(centered * centered, axis=2, keepdims=True)
    inverse = lax.rsqrt(variance + 1e-05)
    normed = centered * inverse
    affine = normed * norm_gain + norm_bias
    sig_affine = jax.nn.sigmoid(affine)
    conv_output = (affine * sig_affine).astype(jnp.bfloat16)
    affine_grad = conv_grad.astype(jnp.float32) * (sig_affine * (1.0 + affine * (1.0 - sig_affine)))
    gain_term = jnp.sum(affine_grad * normed, axis=(0, 1))
    bias_term = jnp.sum(affine_grad, axis=(0, 1))
    normed_grad = affine_grad * norm_gain
    depth_grad = inverse * (
        normed_grad
        - jnp.mean(normed_grad, axis=2, keepdims=True)
        - normed * jnp.mean(normed_grad * normed, axis=2, keepdims=True)
    )
    kernel_term = jnp.stack(
        [
            jnp.sum(depth_grad * glu_view[:, offset : offset + frames], axis=(0, 1))
            for offset in range(taps)
        ]
    )
    kernel_total, gain_total, bias_total = lax.psum(
        (kernel_term, gain_term, bias_term), ("dp", "seq")
    )
    recordings = lax.axis_size("dp")
    kernel_grad = kernel_total / recordings
    gain_grad = gain_total / recordings
    bias_grad = bias_total / recordings
    later = from_behind(depth_grad[:, :span], "seq", -1)
    grad_wide = jnp.concatenate([depth_grad, later], axis=1)
    glu_grad = jnp.zeros((1, frames, channels), jnp.float32)
    for offset in range(taps):
        begin = span - offset
        glu_grad = glu_grad + depth_kernel[offset] * grad_wide[:, begin : begin + frames]
    input_grad = jnp.concatenate(
        [glu_grad * gate_sig, glu_grad * value_half * gate_sig * (1.0 - gate_sig)], axis=2
    ).astype(jnp.bfloat16)
    slope_rows = input_grad[0]
    mixed_grad = jnp.einsum(
        "fc,dc->fd",
        slope_rows,
        lax.all_gather(point_weight, "seq", axis=0, tiled=True),
        preferred_element_type=jnp.float32,
    )
    residual_grad = (context_grad.astype(jnp.float32) + mixed_grad[None]).astype(jnp.bfloat16)
    grad_heads = lax.all_to_all(residual_grad, "seq", split_axis=2, concat_axis=1, tiled=True)
    query_grad, key_grad, value_grad = attend_backward(
        query_heads[0], key_heads[0], value_heads[0], grad_heads[0], context_local, head_count
    )
    query_out, key_out, value_out = (
        lax.all_to_all(query_grad[None], "seq", split_axis=1, concat_axis=2, tiled=True),
        lax.all_to_all(key_grad[None], "seq", split_axis=1, concat_axis=2, tiled=True),
        lax.all_to_all(value_grad[None], "seq", split_axis=1, concat_axis=2, tiled=True),
    )
    return (
        context_out,
        conv_output,
        query_out,
        key_out,
        value_out,
        input_grad,
        residual_grad,
        kernel_grad,
        gain_grad,
        bias_grad,
    )


def solution(mesh):
    in_specs = (
        P("dp", "seq", None),
        P("dp", "seq", None),
        P("dp", "seq", None),
        P("dp", "seq", None),
        P("seq", None),
        P("dp", "seq", None),
        P(),
        P(),
        P(),
        P("dp", "seq", None),
    )
    out_specs = (
        P("dp", "seq", None),
        P("dp", "seq", None),
        P("dp", "seq", None),
        P("dp", "seq", None),
        P("dp", "seq", None),
        P("dp", "seq", None),
        P("dp", "seq", None),
        P(),
        P(),
        P(),
    )
    return jax.shard_map(shards, mesh=mesh, in_specs=in_specs, out_specs=out_specs, check_vma=False)
```

profile of v0, /device:TPU:0, one launch (start us, length us, event | category | flops | bytes accessed | tf_op | source)
XLA Modules:
  0.0 264.9 jit_solution(9525014765251899373)
XLA Ops:
  9.8 2.3 reduce.5
  12.9 4.2 %all-to-all-start = ((bf16[4,2,16384]{2,1,0:T(2,128)(2,1)}), bf16[4,2,16384]{2,1,0:T(2,128)(2,1)S(1)}, u32[]{:S(2)}, u32[]{:S(2)}) async-start(bf16[4,2,16384]{2,1,0:T(2,128)(2,1)} %reshape.213), calls=%async_computation | async-start | bytes 524288 | tf_op jit(solution)/shard_map/all_to_all | solution.py:108
  18.4 2.3 reduce.6
  21.4 2.4 all-to-all-done
  23.9 3.4 %all-to-all-start.1 = ((bf16[4,2,16384]{2,1,0:T(2,128)(2,1)}), bf16[4,2,16384]{2,1,0:T(2,128)(2,1)S(1)}, u32[]{:S(2)}, u32[]{:S(2)}) async-start(bf16[4,2,16384]{2,1,0:T(2,128)(2,1)} %reshape.215), calls=%async_computation.1 | async-start | bytes 524288 | tf_op jit(solution)/shard_map/all_to_all | solution.py:109
  27.7 2.3 reduce.4
  30.7 5.7 %all-to-all-done.1 = bf16[4,2,16384]{2,1,0:T(2,128)(2,1)S(1)} async-done(((bf16[4,2,16384]{2,1,0:T(2,128)(2,1)}), bf16[4,2,16384]{2,1,0:T(2,128)(2,1)S(1)}, u32[]{:S(2)}, u32[]{:S(2)}) %all-to-all-start.1) | async-done | bytes 262176 | tf_op jit(solution)/shard_map/all_to_all | solution.py:109
  36.4 3.4 %all-to-all-start.2 = ((bf16[4,2,16384]{2,1,0:T(2,128)(2,1)}), bf16[4,2,16384]{2,1,0:T(2,128)(2,1)S(1)}, u32[]{:S(2)}, u32[]{:S(2)}) async-start(bf16[4,2,16384]{2,1,0:T(2,128)(2,1)} %reshape.211), calls=%async_computation.2 | async-start | bytes 524288 | tf_op jit(solution)/shard_map/all_to_all | solution.py:110
  42.0 7.0 %all-to-all-done.2 = bf16[4,2,16384]{2,1,0:T(2,128)(2,1)S(1)} async-done(((bf16[4,2,16384]{2,1,0:T(2,128)(2,1)}), bf16[4,2,16384]{2,1,0:T(2,128)(2,1)S(1)}, u32[]{:S(2)}, u32[]{:S(2)}) %all-to-all-start.2) | async-done | bytes 262176 | tf_op jit(solution)/shard_map/all_to_all | solution.py:110
  49.6 3.5 %fusion.114 = (f32[4,512]{1,0:T(4,128)S(1)}, f32[4,512,512]{1,2,0:T(8,128)}) fusion(bf16[512,4,64]{0,2,1:T(8,128)(2,1)S(1)} %reshape_squeeze.15, bf16[512,4,64]{0,2,1:T(8,128)(2,1)S(1)} %reshape_squeeze.16), kind=kOutput, calls=%fused_computation.236 | convolution fusion | flops 137363968 | bytes 4726784 | tf_op jit(solution)/shard_map/while/body/eval_jaxpr/sub | solution.py:20
  53.1 2.8 %fusion.6 = bf16[4,512,512]{1,2,0:T(8,128)(2,1)S(1)} fusion(f32[4,512,512]{1,2,0:T(8,128)} %get-tuple-element.138, f32[4,512]{1,0:T(4,128)S(1)} %get-tuple-element.137), kind=kLoop, calls=%fused_computation.38 | loop fusion | flops 2097152 | bytes 6299648 | tf_op jit(solution)/shard_map/while/body/eval_jaxpr/convert_element_type | solution.py:35
  56.8 2.3 reduce.7
  59.8 3.6 %all-to-all-start.3 = ((bf16[4,2,16384]{2,1,0:T(2,128)(2,1)}), bf16[4,2,16384]{2,1,0:T(2,128)(2,1)S(1)}, u32[]{:S(2)}, u32[]{:S(2)}) async-start(bf16[4,2,16384]{2,1,0:T(2,128)(2,1)} %reshape.217), calls=%async_computation.3 | async-start | bytes 524288 | tf_op jit(solution)/shard_map/all_to_all | solution.py:113
  64.2 5.1 %all-to-all-done.3 = bf16[4,2,16384]{2,1,0:T(2,128)(2,1)S(1)} async-done(((bf16[4,2,16384]{2,1,0:T(2,128)(2,1)}), bf16[4,2,16384]{2,1,0:T(2,128)(2,1)S(1)}, u32[]{:S(2)}, u32[]{:S(2)}) %all-to-all-start.3) | async-done | bytes 262176 | tf_op jit(solution)/shard_map/all_to_all | solution.py:113
  70.8 2.9 %fusion.4 = bf16[1,128,2048]{2,1,0:T(8,128)(2,1)S(1)} fusion(bf16[128,1024]{0,1:T(8,128)(2,1)S(1)} %fusion.105, bf16[1024,2048]{1,0:T(8,128)(2,1)} %all-gather.2.cloned.1.call-done), kind=kOutput, calls=%fused_computation.35 | convolution fusion | flops 537133056 | bytes 4980736 | tf_op jit(solution)/shard_map/dot_general | solution.py:123
  74.5 2.2 collective-permute-start
  78.2 1.8 copy.95
  81.0 3.2 %fusion.111 = (f32[128]{0:T(128)S(1)}, f32[1,128,1024]{2,1,0:T(8,128)S(1)}) fusion(f32[1,158,1024]{2,1,0:T(8,128)S(1)} %convert_element_type.110, f32[1024]{0:T(1024)} %bitcast.253, f32[1024]{0:T(1024)} %bitcast.255, f32[1024]{0:T(1024)S(1)} %bitcast.197, f32[1024]{0:T(1024)S(1)} %bitcast.199, f32[1024]{0:T(1024)S(1)} %bitcast.201, f32[1024]{0:T(1024)} %bitcast.203, ...), kind=kLoop, calls=%fused_computation.233 | loop fusion | flops 8126336 | bytes 16904704 | tf_op jit(solution)/shard_map/reduce_sum | solution.py:138
  89.0 2.6 stack.127
  92.9 43.4 %all-reduce = (f32[1024]{0:T(1024)}, f32[1024]{0:T(1024)}) all-reduce(f32[1024]{0:T(1024)} %get-tuple-element.93, f32[1024]{0:T(1024)} %get-tuple-element.96), channel_id=1, replica_groups=mesh['dp'=8,'seq'=4] {'dp','seq'}, use_global_device_ids=true, to_apply=%region_40.41 | all-reduce | flops 2048 | bytes 16384 | tf_op jit(solution)/shard_map/psum | solution.py:161
  137.6 3.6 %multiply_convert_fusion.1 = (bf16[1,128,1024]{2,1,0:T(8,128)(2,1)S(1)}, f32[1,128,1024]{2,1,0:T(8,128)S(1)}) fusion(bf16[1,128,2048]{2,1,0:T(8,128)(2,1)S(1)} %fusion.4, f32[1,128,1024]{2,1,0:T(8,128)S(1)} %get-tuple-element.99, f32[1024]{0:T(1024)} %bitcast.254, f32[1,30,1024]{2,1,0:T(8,128)S(1)} %collective-permute-done.1, f32[1024]{0:T(1024)} %bitcast.256, ...), kind=kLoop, calls=%fused_computation.210 | loop fusion | flops 12713984 | bytes 1822720 | tf_op jit(solution)/shard_map/convert.7
  141.9 3.7 %fusion.8 = bf16[1,128,1024]{2,1,0:T(8,128)(2,1)S(1)} fusion(bf16[1024,2048]{1,0:T(8,128)(2,1)} %all-gather.2.cloned.1.call-done, bf16[128,1024]{1,0:T(8,128)(2,1)S(1)} %bitcast.164, bf16[128,1024]{1,0:T(8,128)(2,1)S(1)} %bitcast.163, bf16[1,128,1024]{2,1,0:T(8,128)(2,1)} %param.15), kind=kOutput, calls=%fused_computation.74 | convolution fusion | flops 538312704 | bytes 5242880 | tf_op jit(solution)/shard_map/fc,dc->fd/dot_general | solution.py:178
  146.1 3.0 %reduce.8 = bf16[1024,128]{1,0:T(8,128)(2,1)} reduce(bf16[1024,1,128]{2,1,0:T(2,128)(2,1)S(1)} %bitcast.180, bf16[]{:T(256)} %broadcast.119), dimensions={1}, to_apply=%bitcast.135.reduce_sub_computation | reduce | bytes 524290
  150.7 4.3 %all-to-all-start.4 = ((bf16[4,2,16384]{2,1,0:T(2,128)(2,1)}), bf16[4,2,16384]{2,1,0:T(2,128)(2,1)}, u32[]{:S(2)}, u32[]{:S(2)}) async-start(bf16[4,2,16384]{2,1,0:T(2,128)(2,1)} %reshape.219), calls=%async_computation.4 | async-start | bytes 524288 | tf_op jit(solution)/shard_map/all_to_all | solution.py:185
  155.0 61.4 %all-reduce.3.cloned.1.call-done = f32[31,1024]{1,0:T(8,128)} async-done(((f32[31,1024]{1,0:T(8,128)}), f32[31,1024]{1,0:T(8,128)}) %all-reduce.3.cloned.1.call-update) | async-done | bytes 126992 | tf_op jit(solution)/shard_map/psum | solution.py:161
  221.1 3.1 %multiply_convert_fusion = bf16[4,512,512]{1,2,0:T(8,128)(2,1)S(1)} fusion(bf16[512,4,64]{0,2,1:T(8,128)(2,1)S(1)} %reshape_squeeze.18, bf16[512,4,64]{0,2,1:T(8,128)(2,1)S(1)} %copy-done.7, f32[4,512]{1,0:T(4,128)S(1)} %bitcast.288, f32[4,512,512]{1,2,0:T(8,128)} %get-tuple-element.138, f32[4,512]{1,0:T(4,128)S(1)} %copy-done.14), kind=kOutput, calls=%fused_computation.30 | convolution fusion | flops 139460608 | bytes 6832128 | tf_op jit(solution)/shard_map/while/body/eval_jaxpr/qhd,khd->hqk/dot_general | solution.py:69
  224.7 2.3 reduce.11
  227.7 4.0 %all-to-all-start.7 = ((bf16[4,2,16384]{2,1,0:T(2,128)(2,1)}), bf16[4,2,16384]{2,1,0:T(2,128)(2,1)}, u32[]{:S(2)}, u32[]{:S(2)}) async-start(bf16[4,2,16384]{2,1,0:T(2,128)(2,1)} %reshape.225), calls=%async_computation.7 | async-start | bytes 524288 | tf_op jit(solution)/shard_map/all_to_all | solution.py:192
  233.9 2.3 reduce.10
  237.8 3.4 %all-to-all-start.6 = ((bf16[4,2,16384]{2,1,0:T(2,128)(2,1)}), bf16[4,2,16384]{2,1,0:T(2,128)(2,1)S(1)}, u32[]{:S(2)}, u32[]{:S(2)}) async-start(bf16[4,2,16384]{2,1,0:T(2,128)(2,1)} %reshape.223), calls=%async_computation.6 | async-start | bytes 524288 | tf_op jit(solution)/shard_map/all_to_all | solution.py:191
  243.1 2.3 reduce.9
  247.3 3.4 %all-to-all-start.5 = ((bf16[4,2,16384]{2,1,0:T(2,128)(2,1)}), bf16[4,2,16384]{2,1,0:T(2,128)(2,1)S(1)}, u32[]{:S(2)}, u32[]{:S(2)}) async-start(bf16[4,2,16384]{2,1,0:T(2,128)(2,1)} %reshape.221), calls=%async_computation.5 | async-start | bytes 524288 | tf_op jit(solution)/shard_map/all_to_all | solution.py:190
  (118 shorter events, 47.3 us)
Async XLA Ops:
  7.2 20.1 %copy-start.8 = (bf16[1,128,1024]{2,1,0:T(8,128)(2,1)S(1)}, bf16[1,128,1024]{2,1,0:T(8,128)(2,1)}, u32[]{:S(2)}) copy-start(bf16[1,128,1024]{2,1,0:T(8,128)(2,1)} %param.12) | copy-start | bytes 786436
  7.2 63.6 %all-gather.2.cloned.1.call-start = ((), (), s32[]{:S(2)}) async-start(), calls=%async_computation.8 | async-start | bytes 5242880 | tf_op jit(solution)/shard_map/all_gather | solution.py:125
  7.9 31.9 %copy-start.10 = (bf16[1,128,1024]{2,1,0:T(8,128)(2,1)S(1)}, bf16[1,128,1024]{2,1,0:T(8,128)(2,1)}, u32[]{:S(2)}) copy-start(bf16[1,128,1024]{2,1,0:T(8,128)(2,1)} %param.13) | copy-start | bytes 786436
  12.9 11.0 %all-to-all-start = ((bf16[4,2,16384]{2,1,0:T(2,128)(2,1)}), bf16[4,2,16384]{2,1,0:T(2,128)(2,1)S(1)}, u32[]{:S(2)}, u32[]{:S(2)}) async-start(bf16[4,2,16384]{2,1,0:T(2,128)(2,1)} %reshape.213), calls=%async_computation | async-start | bytes 524288 | tf_op jit(solution)/shard_map/all_to_all | solution.py:108
  23.9 12.5 %all-to-all-start.1 = ((bf16[4,2,16384]{2,1,0:T(2,128)(2,1)}), bf16[4,2,16384]{2,1,0:T(2,128)(2,1)S(1)}, u32[]{:S(2)}, u32[]{:S(2)}) async-start(bf16[4,2,16384]{2,1,0:T(2,128)(2,1)} %reshape.215), calls=%async_computation.1 | async-start | bytes 524288 | tf_op jit(solution)/shard_map/all_to_all | solution.py:109
  36.4 12.5 %all-to-all-start.2 = ((bf16[4,2,16384]{2,1,0:T(2,128)(2,1)}), bf16[4,2,16384]{2,1,0:T(2,128)(2,1)S(1)}, u32[]{:S(2)}, u32[]{:S(2)}) async-start(bf16[4,2,16384]{2,1,0:T(2,128)(2,1)} %reshape.211), calls=%async_computation.2 | async-start | bytes 524288 | tf_op jit(solution)/shard_map/all_to_all | solution.py:110
  41.3 11.8 %copy-start.5 = (bf16[512,4,64]{0,2,1:T(8,128)(2,1)}, bf16[512,4,64]{0,2,1:T(8,128)(2,1)S(1)}, u32[]{:S(2)}) copy-start(bf16[512,4,64]{0,2,1:T(8,128)(2,1)S(1)} %reshape_squeeze.15) | copy-start | bytes 786436
  42.0 11.1 %copy-start.4 = (bf16[512,4,64]{0,2,1:T(8,128)(2,1)}, bf16[512,4,64]{0,2,1:T(8,128)(2,1)S(1)}, u32[]{:S(2)}) copy-start(bf16[512,4,64]{0,2,1:T(8,128)(2,1)S(1)} %reshape_squeeze.16) | copy-start | bytes 786436
  49.6 6.3 %copy-start.6 = (bf16[512,4,64]{0,2,1:T(8,128)(2,1)}, bf16[512,4,64]{0,2,1:T(8,128)(2,1)S(1)}, u32[]{:S(2)}) copy-start(bf16[512,4,64]{0,2,1:T(8,128)(2,1)S(1)} %reshape_squeeze.17) | copy-start | bytes 786436
  53.1 3.3 %copy-start.13 = (f32[4,512]{1,0:T(4,128)}, f32[4,512]{1,0:T(4,128)S(1)}, u32[]{:S(2)}) copy-start(f32[4,512]{1,0:T(4,128)S(1)} %get-tuple-element.137) | copy-start | bytes 24580
  55.9 7.6 %copy-start.11 = (f32[31,1024]{1,0:T(8,128)S(1)}, f32[31,1024]{1,0:T(8,128)}, u32[]{:S(2)}) copy-start(f32[31,1024]{1,0:T(8,128)} %param.16) | copy-start | bytes 380932
  59.8 9.4 %all-to-all-start.3 = ((bf16[4,2,16384]{2,1,0:T(2,128)(2,1)}), bf16[4,2,16384]{2,1,0:T(2,128)(2,1)S(1)}, u32[]{:S(2)}, u32[]{:S(2)}) async-start(bf16[4,2,16384]{2,1,0:T(2,128)(2,1)} %reshape.217), calls=%async_computation.3 | async-start | bytes 524288 | tf_op jit(solution)/shard_map/all_to_all | solution.py:113
  63.4 153.0 %all-reduce.3.cloned.1.call-start = ((), (), s32[]{:S(2)}) async-start(), calls=%async_computation.9 | async-start | bytes 262144 | tf_op jit(solution)/shard_map/psum | solution.py:161
  74.5 5.4 %collective-permute-start = (bf16[1,30,1024]{2,1,0:T(8,128)(2,1)}, bf16[1,30,1024]{2,1,0:T(8,128)(2,1)}, u32[]{:S(2)}, u32[]{:S(2)}) collective-permute-start(bf16[1,30,1024]{2,1,0:T(8,128)(2,1)} %slice.448), channel_id=1, source_target_pairs={{0,1},{1,2},{2,3},{4,5},{5,6},{6,7},{8,9},{9,10},{10,11},{12,13},{... | collective-permute-start | bytes 184328 | tf_op jit(solution)/shard_map/ppermute | solution.py:12
  80.9 3.5 %copy-start.9 = (bf16[1,128,1024]{2,1,0:T(8,128)(2,1)S(1)}, bf16[1,128,1024]{2,1,0:T(8,128)(2,1)}, u32[]{:S(2)}) copy-start(bf16[1,128,1024]{2,1,0:T(8,128)(2,1)} %param.19) | copy-start | bytes 786436
  81.0 3.5 %copy-start.12 = (f32[1024]{0:T(1024)S(1)}, f32[1024]{0:T(1024)}, u32[]{:S(2)}) copy-start(f32[1024]{0:T(1024)} %param.17) | copy-start | bytes 12292
  81.0 3.5 %copy-start.15 = (f32[1024]{0:T(1024)S(1)}, f32[1024]{0:T(1024)}, u32[]{:S(2)}) copy-start(f32[1024]{0:T(1024)} %param.18) | copy-start | bytes 12292
  91.6 46.0 %collective-permute-start.1 = (f32[1,30,1024]{2,1,0:T(8,128)}, f32[1,30,1024]{2,1,0:T(8,128)S(1)}, u32[]{:S(2)}, u32[]{:S(2)}) collective-permute-start(f32[1,30,1024]{2,1,0:T(8,128)} %slice.480), channel_id=1, source_target_pairs={{1,0},{2,1},{3,2},{5,4},{6,5},{7,6},{9,8},{10,9},{11,10},{13,12},{... | collective-permute-start | bytes 368648 | tf_op jit(solution)/shard_map/ppermute | solution.py:12
  141.2 0.7 copy-start
  145.6 73.6 %copy-start.2 = (bf16[1,128,1024]{2,1,0:T(8,128)(2,1)}, bf16[1,128,1024]{2,1,0:T(8,128)(2,1)S(1)}, u32[]{:S(2)}) copy-start(bf16[1,128,1024]{2,1,0:T(8,128)(2,1)S(1)} %fusion.8) | copy-start | bytes 786436
  145.7 75.4 %copy-start.14 = (f32[4,512]{1,0:T(4,128)S(1)}, f32[4,512]{1,0:T(4,128)}, u32[]{:S(2)}) copy-start(f32[4,512]{1,0:T(4,128)} %copy-done.13) | copy-start | bytes 24580
  150.7 67.2 %all-to-all-start.4 = ((bf16[4,2,16384]{2,1,0:T(2,128)(2,1)}), bf16[4,2,16384]{2,1,0:T(2,128)(2,1)}, u32[]{:S(2)}, u32[]{:S(2)}) async-start(bf16[4,2,16384]{2,1,0:T(2,128)(2,1)} %reshape.219), calls=%async_computation.4 | async-start | bytes 524288 | tf_op jit(solution)/shard_map/all_to_all | solution.py:185
  219.2 1.9 copy-start.7
  221.1 3.1 %copy-start.3 = (bf16[4,64,512]{2,1,0:T(8,128)(2,1)S(1)}, bf16[4,64,512]{2,1,0:T(8,128)(2,1)}, u32[]{:S(2)}) copy-start(bf16[4,64,512]{2,1,0:T(8,128)(2,1)} %convolution_convert_fusion.3) | copy-start | bytes 786436
  227.7 10.1 %all-to-all-start.7 = ((bf16[4,2,16384]{2,1,0:T(2,128)(2,1)}), bf16[4,2,16384]{2,1,0:T(2,128)(2,1)}, u32[]{:S(2)}, u32[]{:S(2)}) async-start(bf16[4,2,16384]{2,1,0:T(2,128)(2,1)} %reshape.225), calls=%async_computation.7 | async-start | bytes 524288 | tf_op jit(solution)/shard_map/all_to_all | solution.py:192
  233.4 17.2 %copy-start.1 = (bf16[1,128,1024]{2,1,0:T(8,128)(2,1)S(1)}, bf16[1,128,1024]{2,1,0:T(8,128)(2,1)}, u32[]{:S(2)}) copy-start(bf16[1,128,1024]{2,1,0:T(8,128)(2,1)} %copy-done) | copy-start | bytes 786436
  237.8 9.4 %all-to-all-start.6 = ((bf16[4,2,16384]{2,1,0:T(2,128)(2,1)}), bf16[4,2,16384]{2,1,0:T(2,128)(2,1)S(1)}, u32[]{:S(2)}, u32[]{:S(2)}) async-start(bf16[4,2,16384]{2,1,0:T(2,128)(2,1)} %reshape.223), calls=%async_computation.6 | async-start | bytes 524288 | tf_op jit(solution)/shard_map/all_to_all | solution.py:191
  247.3 9.4 %all-to-all-start.5 = ((bf16[4,2,16384]{2,1,0:T(2,128)(2,1)}), bf16[4,2,16384]{2,1,0:T(2,128)(2,1)S(1)}, u32[]{:S(2)}, u32[]{:S(2)}) async-start(bf16[4,2,16384]{2,1,0:T(2,128)(2,1)} %reshape.221), calls=%async_computation.5 | async-start | bytes 524288 | tf_op jit(solution)/shard_map/all_to_all | solution.py:190
Sparse Core Ops, SparseCore 0:
  9.6 43.2 all-gather.1
  91.7 124.6 all-reduce.2
where the time goes:
time: 266 us; the launch traced here: 265 us
  waiting for transfers between devices  85.9 us (32%)
  blocking collectives  43.4 us (16%)
  other arithmetic  38.5 us (14%)
  starting transfers between devices  33.3 us (13%)
  local copies, waits for them, and re-layouts  30.8 us (12%)
  matrix products  18.3 us (7%)
  between operations  14.8 us (6%)
    psum x1, waiting for transfers between devices, shards(): lax.psum((kernel_term, gain_term, bias_term), ('dp', 'seq'))  61.4 us
    psum x1, blocking collectives, shards(): lax.psum((kernel_term, gain_term, bias_term), ('dp', 'seq'))  43.4 us
    unnamed x65, local copies, waits for them, and re-layouts  20.7 us
    unnamed x8, other arithmetic  18.7 us
    all_to_all x1, waiting for transfers between devices, shards(): lax.all_to_all(value_vecs, 'seq', split_axis=2, concat_axis=1, tiled=True)  6.95 us
    all_to_all x1, waiting for transfers between devices, shards(): lax.all_to_all(key_vecs, 'seq', split_axis=2, concat_axis=1, tiled=True)  5.69 us
  transfers between devices with their start and end apart: 12, of which 8 were waited for; matrix products, arithmetic and copies ran while one was open for 23% of the time, Pallas kernels for 0%

commit v1 on v0

--- a/solution.py
+++ b/solution.py
@@ -4,6 +4,13 @@
 from jax.sharding import PartitionSpec as P
 
 HEADS = 16
+
+
+def trade_parts(x, name, split, join):
+    size = lax.axis_size(name)
+    tiles = jnp.stack(jnp.split(x, size, axis=split), axis=0)
+    tiles = lax.all_to_all(tiles, name, split_axis=0, concat_axis=0)
+    return jnp.concatenate(tiles, axis=join)
 
 
 def from_behind(block, axis, distance):
@@ -107,7 +114,7 @@
     query_heads, key_heads, value_heads = (
         lax.all_to_all(queries, "seq", split_axis=2, concat_axis=1, tiled=True),
         lax.all_to_all(key_vecs, "seq", split_axis=2, concat_axis=1, tiled=True),
-        lax.all_to_all(value_vecs, "seq", split_axis=2, concat_axis=1, tiled=True),
+        trade_parts(value_vecs, "seq", 2, 1),
     )
     context_local = attend_forward(query_heads[0], key_heads[0], value_heads[0], head_count)
     context_out = lax.all_to_all(

time: 266 us -> 261 us (0.981)
    all_to_all x1, waiting for transfers between devices: 6.95 us -> 1.15 us  [trade_parts(): tiles = lax.all_to_all(tiles, name, split_axis=0, concat_axis=0)]
    all_to_all x1, waiting for transfers between devices: 2.44 us -> 5.69 us  [shards(): lax.all_to_all(queries, 'seq', split_axis=2, concat_axis=1, tiled=True)]
    unnamed x65 -> x61, local copies, waits for them, and re-layouts: 20.7 us -> 18.3 us
    unnamed x8 -> x7, other arithmetic: 18.7 us -> 16.5 us
  transfers between devices with their start and end apart: 12 -> 12, of which waited for: 8 -> 8; matrix products, arithmetic and copies ran while one was open for 23% -> 22% of each run, Pallas kernels for 0% -> 0%
where the time goes in v1:
time: 261 us; the launch traced here: 260 us
  waiting for transfers between devices  84.9 us (33%)
  blocking collectives  42.6 us (16%)
  other arithmetic  37 us (14%)
  starting transfers between devices  33.1 us (13%)
  local copies, waits for them, and re-layouts  29.3 us (11%)
  matrix products  18.3 us (7%)
  between operations  14.8 us (6%)
    psum x1, waiting for transfers between devices, shards(): lax.psum((kernel_term, gain_term, bias_term), ('dp', 'seq'))  61.2 us
    psum x1, blocking collectives, shards(): lax.psum((kernel_term, gain_term, bias_term), ('dp', 'seq'))  42.6 us
    unnamed x61, local copies, waits for them, and re-layouts  18.3 us
    unnamed x7, other arithmetic  16.5 us
    all_to_all x1, waiting for transfers between devices, shards(): lax.all_to_all(key_vecs, 'seq', split_axis=2, concat_axis=1, tiled=True)  7.3 us
    all_to_all x1, waiting for transfers between devices, shards(): lax.all_to_all(queries, 'seq', split_axis=2, concat_axis=1, tiled=True)  5.69 us
    all_to_all x1, waiting for transfers between devices, shards(): lax.all_to_all(context_local[None], 'seq', split_axis=1, concat_axis=2, t...  5.26 us
  transfers between devices with their start and end apart: 12, of which 8 were waited for; matrix products, arithmetic and copies ran while one was open for 22% of the time, Pallas kernels for 0%

profile of v1, /device:TPU:0, one launch (start us, length us, event | category | flops | bytes accessed | tf_op | source)
XLA Modules:
  0.0 259.9 jit_solution(3094683049089259087)
XLA Ops:
  9.6 4.2 %all-to-all-start = ((bf16[4,1,128,256]{3,2,1,0:T(8,128)(2,1)}), bf16[4,1,128,256]{3,2,1,0:T(8,128)(2,1)S(1)}, u32[]{:S(2)}, u32[]{:S(2)}) async-start(bf16[4,1,128,256]{3,2,1,0:T(8,128)(2,1)} %pad_maximum_fusion.3), calls=%async_computation | async-start | bytes 524288 | tf_op jit(solution)/shard_map/all_to_all | solution.py:12
  15.7 2.3 reduce.4
  19.9 3.4 %all-to-all-start.1 = ((bf16[4,2,16384]{2,1,0:T(2,128)(2,1)}), bf16[4,2,16384]{2,1,0:T(2,128)(2,1)S(1)}, u32[]{:S(2)}, u32[]{:S(2)}) async-start(bf16[4,2,16384]{2,1,0:T(2,128)(2,1)} %reshape.210), calls=%async_computation.1 | async-start | bytes 524288 | tf_op jit(solution)/shard_map/all_to_all | solution.py:115
  23.7 2.3 reduce.5
  26.8 5.7 %all-to-all-done.1 = bf16[4,2,16384]{2,1,0:T(2,128)(2,1)S(1)} async-done(((bf16[4,2,16384]{2,1,0:T(2,128)(2,1)}), bf16[4,2,16384]{2,1,0:T(2,128)(2,1)S(1)}, u32[]{:S(2)}, u32[]{:S(2)}) %all-to-all-start.1) | async-done | bytes 262176 | tf_op jit(solution)/shard_map/all_to_all | solution.py:115
  32.5 3.4 %all-to-all-start.2 = ((bf16[4,2,16384]{2,1,0:T(2,128)(2,1)}), bf16[4,2,16384]{2,1,0:T(2,128)(2,1)S(1)}, u32[]{:S(2)}, u32[]{:S(2)}) async-start(bf16[4,2,16384]{2,1,0:T(2,128)(2,1)} %reshape.212), calls=%async_computation.2 | async-start | bytes 524288 | tf_op jit(solution)/shard_map/all_to_all | solution.py:116
  37.7 7.3 %all-to-all-done.2 = bf16[4,2,16384]{2,1,0:T(2,128)(2,1)S(1)} async-done(((bf16[4,2,16384]{2,1,0:T(2,128)(2,1)}), bf16[4,2,16384]{2,1,0:T(2,128)(2,1)S(1)}, u32[]{:S(2)}, u32[]{:S(2)}) %all-to-all-start.2) | async-done | bytes 262176 | tf_op jit(solution)/shard_map/all_to_all | solution.py:116
  45.7 3.5 %fusion.114 = (f32[4,512]{1,0:T(4,128)S(1)}, f32[4,512,512]{1,2,0:T(8,128)}) fusion(bf16[512,4,64]{0,2,1:T(8,128)(2,1)S(1)} %reshape_squeeze.11, bf16[512,4,64]{0,2,1:T(8,128)(2,1)S(1)} %reshape_squeeze.12), kind=kOutput, calls=%fused_computation.241 | convolution fusion | flops 137363968 | bytes 4726784 | tf_op jit(solution)/shard_map/while/body/eval_jaxpr/sub | solution.py:27
  49.2 2.8 %fusion.6 = bf16[4,512,512]{1,2,0:T(8,128)(2,1)S(1)} fusion(f32[4,512,512]{1,2,0:T(8,128)} %get-tuple-element.142, f32[4,512]{1,0:T(4,128)S(1)} %get-tuple-element.141), kind=kLoop, calls=%fused_computation.38 | loop fusion | flops 2097152 | bytes 6299648 | tf_op jit(solution)/shard_map/while/body/eval_jaxpr/convert_element_type | solution.py:42
  52.9 2.3 reduce.6
  55.9 3.4 %all-to-all-start.3 = ((bf16[4,2,16384]{2,1,0:T(2,128)(2,1)}), bf16[4,2,16384]{2,1,0:T(2,128)(2,1)S(1)}, u32[]{:S(2)}, u32[]{:S(2)}) async-start(bf16[4,2,16384]{2,1,0:T(2,128)(2,1)} %reshape.214), calls=%async_computation.3 | async-start | bytes 524288 | tf_op jit(solution)/shard_map/all_to_all | solution.py:120
  60.1 5.3 %all-to-all-done.3 = bf16[4,2,16384]{2,1,0:T(2,128)(2,1)S(1)} async-done(((bf16[4,2,16384]{2,1,0:T(2,128)(2,1)}), bf16[4,2,16384]{2,1,0:T(2,128)(2,1)S(1)}, u32[]{:S(2)}, u32[]{:S(2)}) %all-to-all-start.3) | async-done | bytes 262176 | tf_op jit(solution)/shard_map/all_to_all | solution.py:120
  66.9 2.9 %fusion.4 = bf16[1,128,2048]{2,1,0:T(8,128)(2,1)S(1)} fusion(bf16[128,1024]{0,1:T(8,128)(2,1)S(1)} %fusion.105, bf16[1024,2048]{1,0:T(8,128)(2,1)} %all-gather.2.cloned.1.call-done), kind=kOutput, calls=%fused_computation.35 | convolution fusion | flops 537133056 | bytes 4980736 | tf_op jit(solution)/shard_map/dot_general | solution.py:130
  70.6 2.1 collective-permute-start
  74.2 1.8 copy.92
  77.1 3.2 %fusion.111 = (f32[128]{0:T(128)S(1)}, f32[1,128,1024]{2,1,0:T(8,128)S(1)}) fusion(f32[1,158,1024]{2,1,0:T(8,128)S(1)} %convert_element_type.110, f32[1024]{0:T(1024)} %bitcast.253, f32[1024]{0:T(1024)} %bitcast.255, f32[1024]{0:T(1024)S(1)} %bitcast.197, f32[1024]{0:T(1024)S(1)} %bitcast.199, f32[1024]{0:T(1024)S(1)} %bitcast.201, f32[1024]{0:T(1024)} %bitcast.203, ...), kind=kLoop, calls=%fused_computation.238 | loop fusion | flops 8126336 | bytes 16904704 | tf_op jit(solution)/shard_map/reduce_sum | solution.py:145
  80.5 1.8 multiply_reduce_fusion.1
  85.0 2.6 stack.147
  88.9 42.6 %all-reduce = (f32[1024]{0:T(1024)}, f32[1024]{0:T(1024)}) all-reduce(f32[1024]{0:T(1024)} %get-tuple-element.93, f32[1024]{0:T(1024)} %get-tuple-element.96), channel_id=1, replica_groups=mesh['dp'=8,'seq'=4] {'dp','seq'}, use_global_device_ids=true, to_apply=%region_40.41 | all-reduce | flops 2048 | bytes 16384 | tf_op jit(solution)/shard_map/psum | solution.py:168
  132.8 3.6 %multiply_convert_fusion.1 = (bf16[1,128,1024]{2,1,0:T(8,128)(2,1)S(1)}, f32[1,128,1024]{2,1,0:T(8,128)S(1)}) fusion(bf16[1,128,2048]{2,1,0:T(8,128)(2,1)S(1)} %fusion.4, f32[1,128,1024]{2,1,0:T(8,128)S(1)} %get-tuple-element.99, f32[1024]{0:T(1024)} %bitcast.254, f32[1,30,1024]{2,1,0:T(8,128)S(1)} %collective-permute-done.1, f32[1024]{0:T(1024)} %bitcast.256, ...), kind=kLoop, calls=%fused_computation.210 | loop fusion | flops 12713984 | bytes 1822720 | tf_op jit(solution)/shard_map/convert.7
  137.1 3.7 %fusion.8 = bf16[1,128,1024]{2,1,0:T(8,128)(2,1)S(1)} fusion(bf16[1024,2048]{1,0:T(8,128)(2,1)} %all-gather.2.cloned.1.call-done, bf16[128,1024]{1,0:T(8,128)(2,1)S(1)} %bitcast.167, bf16[128,1024]{1,0:T(8,128)(2,1)S(1)} %bitcast.166, bf16[1,128,1024]{2,1,0:T(8,128)(2,1)} %param.15), kind=kOutput, calls=%fused_computation.74 | convolution fusion | flops 538312704 | bytes 5242880 | tf_op jit(solution)/shard_map/fc,dc->fd/dot_general | solution.py:185
  141.3 3.0 %reduce.7 = bf16[1024,128]{1,0:T(8,128)(2,1)} reduce(bf16[1024,1,128]{2,1,0:T(2,128)(2,1)S(1)} %bitcast.181, bf16[]{:T(256)} %broadcast.119), dimensions={1}, to_apply=%bitcast.138.reduce_sub_computation | reduce | bytes 524290
  144.2 1.7 reshape.216
  146.0 4.3 %all-to-all-start.4 = ((bf16[4,2,16384]{2,1,0:T(2,128)(2,1)}), bf16[4,2,16384]{2,1,0:T(2,128)(2,1)}, u32[]{:S(2)}, u32[]{:S(2)}) async-start(bf16[4,2,16384]{2,1,0:T(2,128)(2,1)} %reshape.216), calls=%async_computation.4 | async-start | bytes 524288 | tf_op jit(solution)/shard_map/all_to_all | solution.py:192
  150.2 61.2 %all-reduce.3.cloned.1.call-done = f32[31,1024]{1,0:T(8,128)} async-done(((f32[31,1024]{1,0:T(8,128)}), f32[31,1024]{1,0:T(8,128)}) %all-reduce.3.cloned.1.call-update) | async-done | bytes 126992 | tf_op jit(solution)/shard_map/psum | solution.py:168
  216.2 3.1 %multiply_convert_fusion = bf16[4,512,512]{1,2,0:T(8,128)(2,1)S(1)} fusion(bf16[512,4,64]{0,2,1:T(8,128)(2,1)S(1)} %reshape_squeeze.13, bf16[512,4,64]{0,2,1:T(8,128)(2,1)S(1)} %copy-done.7, f32[4,512]{1,0:T(4,128)S(1)} %bitcast.288, f32[4,512,512]{1,2,0:T(8,128)} %get-tuple-element.142, f32[4,512]{1,0:T(4,128)S(1)} %copy-done.14), kind=kOutput, calls=%fused_computation.30 | convolution fusion | flops 139460608 | bytes 6832128 | tf_op jit(solution)/shard_map/while/body/eval_jaxpr/qhd,khd->hqk/dot_general | solution.py:76
  219.7 2.3 reduce.10
  222.7 4.0 %all-to-all-start.7 = ((bf16[4,2,16384]{2,1,0:T(2,128)(2,1)}), bf16[4,2,16384]{2,1,0:T(2,128)(2,1)}, u32[]{:S(2)}, u32[]{:S(2)}) async-start(bf16[4,2,16384]{2,1,0:T(2,128)(2,1)} %reshape.222), calls=%async_computation.7 | async-start | bytes 524288 | tf_op jit(solution)/shard_map/all_to_all | solution.py:199
  228.9 2.3 reduce.9
  232.9 3.4 %all-to-all-start.6 = ((bf16[4,2,16384]{2,1,0:T(2,128)(2,1)}), bf16[4,2,16384]{2,1,0:T(2,128)(2,1)S(1)}, u32[]{:S(2)}, u32[]{:S(2)}) async-start(bf16[4,2,16384]{2,1,0:T(2,128)(2,1)} %reshape.220), calls=%async_computation.6 | async-start | bytes 524288 | tf_op jit(solution)/shard_map/all_to_all | solution.py:198
  238.1 2.3 reduce.8
  242.3 3.4 %all-to-all-start.5 = ((bf16[4,2,16384]{2,1,0:T(2,128)(2,1)}), bf16[4,2,16384]{2,1,0:T(2,128)(2,1)S(1)}, u32[]{:S(2)}, u32[]{:S(2)}) async-start(bf16[4,2,16384]{2,1,0:T(2,128)(2,1)} %reshape.218), calls=%async_computation.5 | async-start | bytes 524288 | tf_op jit(solution)/shard_map/all_to_all | solution.py:197
  (115 shorter events, 44.2 us)
Async XLA Ops:
  7.2 16.2 %copy-start.8 = (bf16[1,128,1024]{2,1,0:T(8,128)(2,1)S(1)}, bf16[1,128,1024]{2,1,0:T(8,128)(2,1)}, u32[]{:S(2)}) copy-start(bf16[1,128,1024]{2,1,0:T(8,128)(2,1)} %param.11) | copy-start | bytes 786436
  7.2 28.7 %copy-start.10 = (bf16[1,128,1024]{2,1,0:T(8,128)(2,1)S(1)}, bf16[1,128,1024]{2,1,0:T(8,128)(2,1)}, u32[]{:S(2)}) copy-start(bf16[1,128,1024]{2,1,0:T(8,128)(2,1)} %param.13) | copy-start | bytes 786436
  7.2 59.7 %all-gather.2.cloned.1.call-start = ((), (), s32[]{:S(2)}) async-start(), calls=%async_computation.8 | async-start | bytes 5242880 | tf_op jit(solution)/shard_map/all_gather | solution.py:132
  9.6 10.3 %all-to-all-start = ((bf16[4,1,128,256]{3,2,1,0:T(8,128)(2,1)}), bf16[4,1,128,256]{3,2,1,0:T(8,128)(2,1)S(1)}, u32[]{:S(2)}, u32[]{:S(2)}) async-start(bf16[4,1,128,256]{3,2,1,0:T(8,128)(2,1)} %pad_maximum_fusion.3), calls=%async_computation | async-start | bytes 524288 | tf_op jit(solution)/shard_map/all_to_all | solution.py:12
  19.9 12.6 %all-to-all-start.1 = ((bf16[4,2,16384]{2,1,0:T(2,128)(2,1)}), bf16[4,2,16384]{2,1,0:T(2,128)(2,1)S(1)}, u32[]{:S(2)}, u32[]{:S(2)}) async-start(bf16[4,2,16384]{2,1,0:T(2,128)(2,1)} %reshape.210), calls=%async_computation.1 | async-start | bytes 524288 | tf_op jit(solution)/shard_map/all_to_all | solution.py:115
  32.5 12.5 %all-to-all-start.2 = ((bf16[4,2,16384]{2,1,0:T(2,128)(2,1)}), bf16[4,2,16384]{2,1,0:T(2,128)(2,1)S(1)}, u32[]{:S(2)}, u32[]{:S(2)}) async-start(bf16[4,2,16384]{2,1,0:T(2,128)(2,1)} %reshape.212), calls=%async_computation.2 | async-start | bytes 524288 | tf_op jit(solution)/shard_map/all_to_all | solution.py:116
  37.0 14.9 %copy-start.6 = (bf16[512,4,64]{0,2,1:T(8,128)(2,1)}, bf16[512,4,64]{0,2,1:T(8,128)(2,1)S(1)}, u32[]{:S(2)}) copy-start(bf16[512,4,64]{0,2,1:T(8,128)(2,1)S(1)} %reshape_squeeze_reshape.4) | copy-start | bytes 786436
  37.7 11.5 %copy-start.5 = (bf16[512,4,64]{0,2,1:T(8,128)(2,1)}, bf16[512,4,64]{0,2,1:T(8,128)(2,1)S(1)}, u32[]{:S(2)}) copy-start(bf16[512,4,64]{0,2,1:T(8,128)(2,1)S(1)} %reshape_squeeze.11) | copy-start | bytes 786436
  45.7 3.5 %copy-start.4 = (bf16[512,4,64]{0,2,1:T(8,128)(2,1)}, bf16[512,4,64]{0,2,1:T(8,128)(2,1)S(1)}, u32[]{:S(2)}) copy-start(bf16[512,4,64]{0,2,1:T(8,128)(2,1)S(1)} %reshape_squeeze.12) | copy-start | bytes 786436
  49.1 3.3 %copy-start.13 = (f32[4,512]{1,0:T(4,128)}, f32[4,512]{1,0:T(4,128)S(1)}, u32[]{:S(2)}) copy-start(f32[4,512]{1,0:T(4,128)S(1)} %get-tuple-element.141) | copy-start | bytes 24580
  51.9 7.4 %copy-start.11 = (f32[31,1024]{1,0:T(8,128)S(1)}, f32[31,1024]{1,0:T(8,128)}, u32[]{:S(2)}) copy-start(f32[31,1024]{1,0:T(8,128)} %param.16) | copy-start | bytes 380932
  55.9 9.4 %all-to-all-start.3 = ((bf16[4,2,16384]{2,1,0:T(2,128)(2,1)}), bf16[4,2,16384]{2,1,0:T(2,128)(2,1)S(1)}, u32[]{:S(2)}, u32[]{:S(2)}) async-start(bf16[4,2,16384]{2,1,0:T(2,128)(2,1)} %reshape.214), calls=%async_computation.3 | async-start | bytes 524288 | tf_op jit(solution)/shard_map/all_to_all | solution.py:120
  59.3 152.1 %all-reduce.3.cloned.1.call-start = ((), (), s32[]{:S(2)}) async-start(), calls=%async_computation.9 | async-start | bytes 262144 | tf_op jit(solution)/shard_map/psum | solution.py:168
  70.6 5.4 %collective-permute-start = (bf16[1,30,1024]{2,1,0:T(8,128)(2,1)}, bf16[1,30,1024]{2,1,0:T(8,128)(2,1)}, u32[]{:S(2)}, u32[]{:S(2)}) collective-permute-start(bf16[1,30,1024]{2,1,0:T(8,128)(2,1)} %slice.448), channel_id=1, source_target_pairs={{0,1},{1,2},{2,3},{4,5},{5,6},{6,7},{8,9},{9,10},{10,11},{12,13},{... | collective-permute-start | bytes 184328 | tf_op jit(solution)/shard_map/ppermute | solution.py:19
  77.0 3.5 %copy-start.9 = (bf16[1,128,1024]{2,1,0:T(8,128)(2,1)S(1)}, bf16[1,128,1024]{2,1,0:T(8,128)(2,1)}, u32[]{:S(2)}) copy-start(bf16[1,128,1024]{2,1,0:T(8,128)(2,1)} %param.19) | copy-start | bytes 786436
  77.0 3.5 %copy-start.12 = (f32[1024]{0:T(1024)S(1)}, f32[1024]{0:T(1024)}, u32[]{:S(2)}) copy-start(f32[1024]{0:T(1024)} %param.17) | copy-start | bytes 12292
  77.0 3.5 %copy-start.15 = (f32[1024]{0:T(1024)S(1)}, f32[1024]{0:T(1024)}, u32[]{:S(2)}) copy-start(f32[1024]{0:T(1024)} %param.18) | copy-start | bytes 12292
  87.6 45.2 %collective-permute-start.1 = (f32[1,30,1024]{2,1,0:T(8,128)}, f32[1,30,1024]{2,1,0:T(8,128)S(1)}, u32[]{:S(2)}, u32[]{:S(2)}) collective-permute-start(f32[1,30,1024]{2,1,0:T(8,128)} %slice.480), channel_id=1, source_target_pairs={{1,0},{2,1},{3,2},{5,4},{6,5},{7,6},{9,8},{10,9},{11,10},{13,12},{... | collective-permute-start | bytes 368648 | tf_op jit(solution)/shard_map/ppermute | solution.py:19
  136.4 0.7 copy-start
  140.9 73.4 %copy-start.2 = (bf16[1,128,1024]{2,1,0:T(8,128)(2,1)}, bf16[1,128,1024]{2,1,0:T(8,128)(2,1)S(1)}, u32[]{:S(2)}) copy-start(bf16[1,128,1024]{2,1,0:T(8,128)(2,1)S(1)} %fusion.8) | copy-start | bytes 786436
  140.9 75.3 %copy-start.14 = (f32[4,512]{1,0:T(4,128)S(1)}, f32[4,512]{1,0:T(4,128)}, u32[]{:S(2)}) copy-start(f32[4,512]{1,0:T(4,128)} %copy-done.13) | copy-start | bytes 24580
  146.0 67.1 %all-to-all-start.4 = ((bf16[4,2,16384]{2,1,0:T(2,128)(2,1)}), bf16[4,2,16384]{2,1,0:T(2,128)(2,1)}, u32[]{:S(2)}, u32[]{:S(2)}) async-start(bf16[4,2,16384]{2,1,0:T(2,128)(2,1)} %reshape.216), calls=%async_computation.4 | async-start | bytes 524288 | tf_op jit(solution)/shard_map/all_to_all | solution.py:192
  214.2 1.9 copy-start.7
  216.1 3.1 %copy-start.3 = (bf16[4,64,512]{2,1,0:T(8,128)(2,1)S(1)}, bf16[4,64,512]{2,1,0:T(8,128)(2,1)}, u32[]{:S(2)}) copy-start(bf16[4,64,512]{2,1,0:T(8,128)(2,1)} %convolution_convert_fusion.2) | copy-start | bytes 786436
  222.7 10.1 %all-to-all-start.7 = ((bf16[4,2,16384]{2,1,0:T(2,128)(2,1)}), bf16[4,2,16384]{2,1,0:T(2,128)(2,1)}, u32[]{:S(2)}, u32[]{:S(2)}) async-start(bf16[4,2,16384]{2,1,0:T(2,128)(2,1)} %reshape.222), calls=%async_computation.7 | async-start | bytes 524288 | tf_op jit(solution)/shard_map/all_to_all | solution.py:199
  228.5 17.2 %copy-start.1 = (bf16[1,128,1024]{2,1,0:T(8,128)(2,1)S(1)}, bf16[1,128,1024]{2,1,0:T(8,128)(2,1)}, u32[]{:S(2)}) copy-start(bf16[1,128,1024]{2,1,0:T(8,128)(2,1)} %copy-done) | copy-start | bytes 786436
  232.9 9.4 %all-to-all-start.6 = ((bf16[4,2,16384]{2,1,0:T(2,128)(2,1)}), bf16[4,2,16384]{2,1,0:T(2,128)(2,1)S(1)}, u32[]{:S(2)}, u32[]{:S(2)}) async-start(bf16[4,2,16384]{2,1,0:T(2,128)(2,1)} %reshape.220), calls=%async_computation.6 | async-start | bytes 524288 | tf_op jit(solution)/shard_map/all_to_all | solution.py:198
  242.3 9.4 %all-to-all-start.5 = ((bf16[4,2,16384]{2,1,0:T(2,128)(2,1)}), bf16[4,2,16384]{2,1,0:T(2,128)(2,1)S(1)}, u32[]{:S(2)}, u32[]{:S(2)}) async-start(bf16[4,2,16384]{2,1,0:T(2,128)(2,1)} %reshape.218), calls=%async_computation.5 | async-start | bytes 524288 | tf_op jit(solution)/shard_map/all_to_all | solution.py:197
Sparse Core Ops, SparseCore 0:
  9.6 42.7 all-gather.1
  87.8 123.6 all-reduce.2
